TPU v7x, 32 devices: a whole 2x2x4 slice. The times are simulated.
32 devices in a mesh: grp: 2 (over y), seq: 4 (over x, core), lab: 4 (over z).
Axes of the slice: x: 2, y: 2, z: 4, core: 2. Of those that a mesh axis runs over, the one named last changes fastest.
Arguments:
- hidden: bfloat16 [6144, 4096], P(('grp', 'seq'), 'lab'), parts along dimension 0, may hold values from -6 to 6
- proj_weight: bfloat16 [4096, 256], P('lab'), may hold values from -0.09375 to 0.09375
- queries: bfloat16 [9216, 256], P('lab'), may hold values from -0.25 to 0.25
- code_weight: bfloat16 [9216, 256], P('lab'), may hold values from -4 to 4
- code_bias: float32 [9216], P('lab'), may hold values from -0.5 to 0.5
- labels: int32 [4, 9216], P('grp', 'lab'), parts along dimension 0, may hold values 0 or 1
- code_counts: int32 [8, 9216], P(('grp', 'seq'), 'lab'), parts along dimension 0, may hold values from 0 to 119, as said below
Outputs:
- note_loss: float32 [4], P('grp'), parts along dimension 0
- grad_hidden: bfloat16 [6144, 4096], P(('grp', 'seq'), 'lab'), parts along dimension 0
- grad_proj: bfloat16 [8192, 256], P(('grp', 'lab', 'seq')), parts along dimension 0
- grad_queries: bfloat16 [18432, 256], P(('grp', 'lab', 'seq')), parts along dimension 0
- grad_code_weight: bfloat16 [18432, 256], P(('grp', 'lab', 'seq')), parts along dimension 0
- grad_bias: float32 [18432], P(('grp', 'lab')), parts along dimension 0
There are 2 independent parts, one for each index of `grp`. A program takes and returns all parts, laid end to end along the dimension named above; an argument that names none is the same for every part. Nothing has to cross between parts.
Inputs may be any that keep to these rules, and one draw needn't show every extreme that they name: `code_counts`: entry (i, c) counts the occurrences of code c in the part of the training corpus read by loader i.
All inputs are finite; a program needn't handle non-finite values. No bound on the sum of `labels` on one device may be relied on, other than what follows from the above.
Results may differ from a plain program's by a relative error of at most 0.025.
Values may be sent and summed in bfloat16 or wider, within the bound.
A program may use at most 64 MiB of HBM per device.

v0:
```python
import math

import jax
import jax.numpy as jnp
from jax import lax
from jax.sharding import PartitionSpec as P

balance_beta = 0.9999


def focal_loss(logit, target):
    prob = jax.nn.sigmoid(logit)
    return -(
        target * (1.0 - prob) * (1.0 - prob) * jax.nn.log_sigmoid(logit)
        + (1.0 - target) * prob * prob * jax.nn.log_sigmoid(-logit)
    )


def rounded(value):
    return lax.optimization_barrier(value.astype(jnp.bfloat16)).astype(jnp.float32)


def per_device(hidden, proj_weight, queries, code_weight, code_bias, labels, code_counts):
    lab_count = lax.axis_size("lab")
    seq_count = lax.axis_size("seq")
    note_count = labels.shape[0]
    all_codes = queries.shape[0] * lab_count
    pre_part = lax.psum_scatter(
        jnp.dot(hidden, proj_weight, preferred_element_type=jnp.float32).astype(jnp.bfloat16),
        "lab",
        scatter_dimension=0,
        tiled=True,
    ).astype(jnp.float32)
    latent_share = jnp.tanh(pre_part).astype(jnp.bfloat16)
    latent = lax.all_gather(latent_share, "lab", axis=0, tiled=True)
    scores = jnp.einsum("te,ce->tc", latent, queries, preferred_element_type=jnp.float32)
    values = jnp.einsum("te,ce->tc", latent, code_weight, preferred_element_type=jnp.float32)
    weights = jnp.exp(scores)
    note_here = lax.axis_index("seq") * note_count // seq_count
    note_pick = (jnp.arange(note_count, dtype=jnp.int32) == note_here).astype(jnp.float32)[:, None]
    den_local = jnp.sum(weights, 0)[None, :]
    num_local = jnp.sum(weights * values, 0)[None, :]
    counts_local = jnp.sum(code_counts.astype(jnp.float32), 0)
    denominator, numerator, counted = (
        lax.psum((note_pick * den_local).astype(jnp.bfloat16), "seq").astype(jnp.float32),
        lax.psum((note_pick * num_local).astype(jnp.bfloat16), "seq").astype(jnp.float32),
        lax.psum(counts_local.astype(jnp.bfloat16), "seq").astype(jnp.float32),
    )
    mean_value = numerator / denominator
    logits = mean_value + code_bias[None, :]
    occurrences = 1.0 + counted
    class_weight = (1.0 - balance_beta) / -jnp.expm1(occurrences * math.log(balance_beta))
    targets = labels.astype(jnp.float32)
    focal_value, pullback = jax.vjp(lambda point: focal_loss(point, targets), logits)
    focal_grad = pullback(jnp.ones_like(logits))[0]
    weight_total, weighted_loss = lax.psum(
        (jnp.sum(class_weight), jnp.sum(focal_value * class_weight[None, :], 1)), "lab"
    )
    factor = all_codes / weight_total
    note_loss = factor * weighted_loss
    logit_grad = factor * class_weight[None, :] * focal_grad
    grad_bias = jnp.sum(logit_grad, 0)
    grad_here = jnp.sum(note_pick * logit_grad, 0)[None, :]
    den_here = jnp.sum(note_pick * denominator, 0)[None, :]
    mean_here = jnp.sum(note_pick * mean_value, 0)[None, :]
    value_part = weights / den_here * grad_here
    score_part = value_part * (values - mean_here)
    value_grad = value_part.astype(jnp.bfloat16)
    score_grad = score_part.astype(jnp.bfloat16)
    first = jnp.dot(score_grad, queries, preferred_element_type=jnp.float32)
    grad_share = lax.psum_scatter(
        (first + jnp.dot(value_grad, code_weight, preferred_element_type=jnp.float32)).astype(
            jnp.bfloat16
        ),
        "lab",
        scatter_dimension=0,
        tiled=True,
    ).astype(jnp.float32)
    share_wide = latent_share.astype(jnp.float32)
    pre_share_grad = (grad_share * (1.0 - share_wide * share_wide)).astype(jnp.bfloat16)
    pre_grad = lax.all_gather(pre_share_grad, "lab", axis=0, tiled=True)
    grad_hidden = jnp.einsum(
        "te,de->td", pre_grad, proj_weight, preferred_element_type=jnp.float32
    ).astype(jnp.bfloat16)
    proj_part = jnp.einsum("td,te->de", hidden, pre_grad, preferred_element_type=jnp.float32)
    query_part = jnp.einsum("tc,te->ce", score_grad, latent, preferred_element_type=jnp.float32)
    weight_part = jnp.einsum("tc,te->ce", value_grad, latent, preferred_element_type=jnp.float32)
    query_sum, weight_sum, proj_sum = (
        lax.psum_scatter(
            rounded(query_part).astype(jnp.bfloat16), "seq", scatter_dimension=0, tiled=True
        ).astype(jnp.float32),
        lax.psum_scatter(
            rounded(weight_part).astype(jnp.bfloat16), "seq", scatter_dimension=0, tiled=True
        ).astype(jnp.float32),
        lax.psum_scatter(
            rounded(proj_part).astype(jnp.bfloat16), "seq", scatter_dimension=0, tiled=True
        ).astype(jnp.float32),
    )
    return (
        note_loss,
        grad_hidden,
        proj_sum.astype(jnp.bfloat16),
        query_sum.astype(jnp.bfloat16),
        weight_sum.astype(jnp.bfloat16),
        grad_bias,
    )


def solution(mesh):
    placed = (
        P(("grp", "seq"), "lab"),
        P("lab", None),
        P("lab", None),
        P("lab", None),
        P("lab"),
        P("grp", "lab"),
        P(("grp", "seq"), "lab"),
    )
    return jax.shard_map(
        per_device,
        mesh=mesh,
        in_specs=placed,
        out_specs=(
            P("grp"),
            P(("grp", "seq"), "lab"),
            P(("grp", "lab", "seq"), None),
            P(("grp", "lab", "seq"), None),
            P(("grp", "lab", "seq"), None),
            P(("grp", "lab")),
        ),
        check_vma=False,
    )
```

profile of v0, /device:TPU:0, one launch (start us, length us, event | category | flops | bytes accessed | tf_op | source)
XLA Modules:
  0.0 211.3 jit_solution(14797629354521924660)
XLA Ops:
  7.2 0.0 copy-start
  7.2 0.0 reduce-scatter.6.cloned.1.call-start
  7.2 1.4 copy-done
  8.6 2.4 %convolution_convert_fusion.4 = bf16[768,256]{1,0:T(8,128)(2,1)} fusion(bf16[768,1024]{1,0:T(8,128)(2,1)S(1)} %copy-done, bf16[1024,256]{1,0:T(8,128)(2,1)} %param.9), kind=kOutput, calls=%fused_computation.11 | convolution fusion | flops 402849792 | bytes 2490368 | tf_op jit(solution)/shard_map/dot_general | solution.py:29
  10.9 0.0 reduce-scatter.6.cloned.1.call-update
  11.0 0.0 reduce-scatter.8.cloned.1.call-start
  11.0 0.7 convert_reduce_fusion
  11.8 22.6 %reduce-scatter.6.cloned.1.call-done = bf16[192,256]{1,0:T(8,128)(2,1)} async-done(((bf16[768,256]{1,0:T(8,128)(2,1)}), bf16[192,256]{1,0:T(8,128)(2,1)}) %reduce-scatter.6.cloned.1.call-update) | async-done | bytes 98320 | tf_op jit(solution)/shard_map/reduce_scatter | solution.py:28
  34.4 0.9 tanh_convert_fusion
  35.3 14.8 %all_gather.6 = bf16[768,256]{1,0:T(8,128)(2,1)S(1)} all-gather(bf16[192,256]{1,0:T(8,128)(2,1)S(1)} %tanh_convert_fusion), channel_id=1, replica_groups=mesh['grp'=2,'seq'=4,'lab'=4] {'lab'}, dimensions={0}, use_global_device_ids=true | all-gather | bytes 491520 | tf_op jit(solution)/shard_map/all_gather | solution.py:35
  50.1 0.0 copy-start.4
  50.2 2.5 %fusion.17 = f32[768,2304]{1,0:T(8,128)S(1)} fusion(bf16[768,256]{1,0:T(8,128)(2,1)S(1)} %all_gather.6, bf16[2304,256]{1,0:T(8,128)(2,1)} %param.10), kind=kOutput, calls=%fused_computation.52 | convolution fusion | flops 905969664 | bytes 8650752 | tf_op jit(solution)/shard_map/te,ce->tc/dot_general | solution.py:36
  52.6 0.0 copy-done.4
  52.6 0.0 copy-start.1
  52.7 0.0 copy-start.8
  52.7 0.0 copy-start.9
  52.7 4.8 %multiply_reduce_fusion = (f32[2304]{0:T(1024)S(1)}, f32[2304]{0:T(1024)S(1)}, f32[768,2304]{1,0:T(8,128)}) fusion(f32[768,2304]{1,0:T(8,128)S(1)} %fusion.17, bf16[768,256]{1,0:T(8,128)(2,1)S(1)} %all_gather.6, bf16[2304,256]{1,0:T(8,128)(2,1)S(1)} %copy-done.4), kind=kOutput, calls=%fused_computation.2 | convolution fusion | flops 911273472 | bytes 15747072 | tf_op jit(solution)/shard_map/te,ce->tc/dot_general | solution.py:37
  57.5 0.2 copy-done.1
  57.6 0.1 multiply_convert_fusion.3
  57.7 10.3 %all-reduce = (bf16[2304]{0:T(1024)(128)(2,1)S(1)}, bf16[2,2304]{1,0:T(2,128)(2,1)S(1)}, bf16[2,2304]{1,0:T(2,128)(2,1)S(1)}) all-reduce(bf16[2304]{0:T(1024)(128)(2,1)S(1)} %convert_reduce_fusion, bf16[2,2304]{1,0:T(2,128)(2,1)S(1)} %get-tuple-element.39, ...), channel_id=1, replica_groups=mesh['grp'=2,'seq'=4,'lab'=4] {'seq'}, use_global_device_ids=true, to_apply=%region_0.0 | all-reduce | flops 11520 | bytes 46080 | tf_op jit(solution)/shard_map/psum | solution.py:47
  68.0 0.6 negate_divide_fusion
  68.6 9.0 %psum.36 = f32[]{:T(128)} all-reduce(f32[]{:T(128)} %get-tuple-element.37), channel_id=1, replica_groups=mesh['grp'=2,'seq'=4,'lab'=4] {'lab'}, use_global_device_ids=true, to_apply=%region_2.3 | all-reduce | flops 1 | bytes 8 | tf_op jit(solution)/shard_map/psum | solution.py:56
  78.3 0.0 copy-done.8
  78.3 0.0 copy-done.9
  78.3 0.2 fusion.14
  78.5 0.8 fusion.16
  79.4 0.0 copy-start.5
  79.4 6.0 %fusion = (bf16[768,2304]{1,0:T(8,128)(2,1)S(1)}, bf16[768,2304]{1,0:T(8,128)(2,1)S(1)}) fusion(f32[2304]{0:T(1024)S(1)} %get-tuple-element.23, f32[2304]{0:T(1024)S(1)} %get-tuple-element.26, f32[768,2304]{1,0:T(8,128)} %copy-done.1, f32[768,2304]{1,0:T(8,128)} %get-tuple-element.40, f32[2304]{0:T(1024)S(1)} %get-tuple-element.28), kind=kLoop, calls=%fused_computation.6 | loop fusion | flops 10616832 | bytes 21261312 | tf_op jit(solution)/shard_map/convert_element_type | solution.py:68
  85.4 0.0 copy-start.3
  85.4 0.0 copy-start.2
  85.4 1.8 copy-done.3
  87.2 0.0 copy-done.5
  87.2 1.1 fusion.18
  88.3 0.0 copy-done.2
  88.3 0.0 copy-start.7
  88.3 1.8 fusion.1
  90.2 0.0 reduce-scatter.8.cloned.1.call-update
  90.2 0.0 reduce-scatter.10.cloned.1.call-start
  90.2 20.2 %reduce-scatter.8.cloned.1.call-done = bf16[192,256]{1,0:T(8,128)(2,1)} async-done(((bf16[768,256]{1,0:T(8,128)(2,1)}), bf16[192,256]{1,0:T(8,128)(2,1)}) %reduce-scatter.8.cloned.1.call-update) | async-done | bytes 98320 | tf_op jit(solution)/shard_map/reduce_scatter | solution.py:71
  110.4 0.0 copy-done.7
  110.4 0.9 multiply_convert_fusion.1
  111.3 14.8 %all_gather.7 = bf16[768,256]{1,0:T(8,128)(2,1)S(1)} all-gather(bf16[192,256]{1,0:T(8,128)(2,1)S(1)} %multiply_convert_fusion.1), channel_id=1, replica_groups=mesh['grp'=2,'seq'=4,'lab'=4] {'lab'}, dimensions={0}, use_global_device_ids=true | all-gather | bytes 491520 | tf_op jit(solution)/shard_map/all_gather | solution.py:81
  126.1 1.4 fusion.2
  127.6 0.0 reduce-scatter.10.cloned.1.call-update
  127.6 0.0 reduce-scatter.12.cloned.1.call-start
  127.6 4.2 %convolution_convert_fusion.1 = bf16[2304,256]{1,0:T(8,128)(2,1)} fusion(bf16[768,2304]{1,0:T(8,128)(2,1)} %copy-done.3, bf16[768,256]{1,0:T(8,128)(2,1)S(1)} %all_gather.6), kind=kOutput, calls=%fused_computation.5 | convolution fusion | flops 906559488 | bytes 5111808 | tf_op jit(solution)/shard_map/tc,te->ce/dot_general | solution.py:86
  131.8 0.0 reduce-scatter.12.cloned.1.call-update
  131.8 0.0 copy-start.6
  131.8 0.0 reduce-scatter.14.cloned.1.call-start
  131.9 4.3 %convolution_convert_fusion = bf16[2304,256]{1,0:T(8,128)(2,1)} fusion(bf16[768,2304]{1,0:T(8,128)(2,1)} %copy-done.2, bf16[768,256]{1,0:T(8,128)(2,1)S(1)} %all_gather.6), kind=kOutput, calls=%fused_computation.4 | convolution fusion | flops 906559488 | bytes 5111808 | tf_op jit(solution)/shard_map/tc,te->ce/dot_general | solution.py:87
  136.2 0.0 reduce-scatter.14.cloned.1.call-update
  136.2 8.4 %psum.39 = f32[2]{0:T(128)S(1)} all-reduce(f32[2]{0:T(128)S(1)} %get-tuple-element.27), channel_id=1, replica_groups=mesh['grp'=2,'seq'=4,'lab'=4] {'lab'}, use_global_device_ids=true, to_apply=%region_9.11 | all-reduce | flops 2 | bytes 16 | tf_op jit(solution)/shard_map/psum | solution.py:56
  144.6 0.5 broadcast_multiply_fusion.1
  145.1 0.0 copy-done.6
  145.1 1.7 convolution_convert_fusion.2
  146.8 0.3 reduce-scatter.10.cloned.1.call-done
  147.1 1.7 copy.13
  148.8 27.2 %reduce-scatter.12.cloned.1.call-done = bf16[576,256]{1,0:T(8,128)(2,1)} async-done(((bf16[2304,256]{1,0:T(8,128)(2,1)}), bf16[576,256]{1,0:T(8,128)(2,1)}) %reduce-scatter.12.cloned.1.call-update) | async-done | bytes 294928 | tf_op jit(solution)/shard_map/reduce_scatter | solution.py:89
  176.0 28.7 %reduce-scatter.14.cloned.1.call-done = bf16[576,256]{1,0:T(8,128)(2,1)} async-done(((bf16[2304,256]{1,0:T(8,128)(2,1)}), bf16[576,256]{1,0:T(8,128)(2,1)}) %reduce-scatter.14.cloned.1.call-update) | async-done | bytes 294928 | tf_op jit(solution)/shard_map/reduce_scatter | solution.py:92
  (2 shorter events, 0.0 us)
Async XLA Ops:
  7.2 1.4 copy-start
  7.2 27.2 %reduce-scatter.6.cloned.1.call-start = ((), (), s32[]{:S(2)}) async-start(), calls=%async_computation.5 | async-start | bytes 491520 | tf_op jit(solution)/shard_map/reduce_scatter | solution.py:28
  11.0 99.4 %reduce-scatter.8.cloned.1.call-start = ((), (), s32[]{:S(2)}) async-start(), calls=%async_computation.6 | async-start | bytes 491520 | tf_op jit(solution)/shard_map/reduce_scatter | solution.py:71
  50.1 2.5 %copy-start.4 = (bf16[2304,256]{1,0:T(8,128)(2,1)S(1)}, bf16[2304,256]{1,0:T(8,128)(2,1)}, u32[]{:S(2)}) copy-start(bf16[2304,256]{1,0:T(8,128)(2,1)} %param.11) | copy-start | bytes 3538948
  52.6 5.0 %copy-start.1 = (f32[768,2304]{1,0:T(8,128)}, f32[768,2304]{1,0:T(8,128)S(1)}, u32[]{:S(2)}) copy-start(f32[768,2304]{1,0:T(8,128)S(1)} %fusion.17) | copy-start | bytes 21233668
  52.7 25.6 %copy-start.8 = (s32[2,2304]{1,0:T(2,128)S(1)}, s32[2,2304]{1,0:T(2,128)}, u32[]{:S(2)}) copy-start(s32[2,2304]{1,0:T(2,128)} %param.13) | copy-start | bytes 55300
  52.7 25.6 %copy-start.9 = (f32[2304]{0:T(1024)S(1)}, f32[2304]{0:T(1024)}, u32[]{:S(2)}) copy-start(f32[2304]{0:T(1024)} %param.12) | copy-start | bytes 27652
  79.4 7.9 %copy-start.5 = (bf16[2304,256]{1,0:T(8,128)(2,1)S(1)}, bf16[2304,256]{1,0:T(8,128)(2,1)}, u32[]{:S(2)}) copy-start(bf16[2304,256]{1,0:T(8,128)(2,1)} %param.10) | copy-start | bytes 3538948
  85.4 1.8 copy-start.3
  85.4 2.9 %copy-start.2 = (bf16[768,2304]{1,0:T(8,128)(2,1)}, bf16[768,2304]{1,0:T(8,128)(2,1)S(1)}, u32[]{:S(2)}) copy-start(bf16[768,2304]{1,0:T(8,128)(2,1)S(1)} %get-tuple-element.34) | copy-start | bytes 10616836
  88.3 22.1 %copy-start.7 = (bf16[192,256]{1,0:T(8,128)(2,1)S(1)}, bf16[192,256]{1,0:T(8,128)(2,1)}, u32[]{:S(2)}) copy-start(bf16[192,256]{1,0:T(8,128)(2,1)} %reduce-scatter.6.cloned.1.call-done) | copy-start | bytes 294916
  90.2 56.9 %reduce-scatter.10.cloned.1.call-start = ((), (), s32[]{:S(2)}) async-start(), calls=%async_computation.7 | async-start | bytes 655360 | tf_op jit(solution)/shard_map/reduce_scatter | solution.py:95
  127.6 48.4 %reduce-scatter.12.cloned.1.call-start = ((), (), s32[]{:S(2)}) async-start(), calls=%async_computation.8 | async-start | bytes 1474560 | tf_op jit(solution)/shard_map/reduce_scatter | solution.py:89
  131.8 13.3 %copy-start.6 = (bf16[1024,256]{1,0:T(8,128)(2,1)S(1)}, bf16[1024,256]{1,0:T(8,128)(2,1)}, u32[]{:S(2)}) copy-start(bf16[1024,256]{1,0:T(8,128)(2,1)} %param.9) | copy-start | bytes 1572868
  131.8 72.9 %reduce-scatter.14.cloned.1.call-start = ((), (), s32[]{:S(2)}) async-start(), calls=%async_computation.9 | async-start | bytes 1474560 | tf_op jit(solution)/shard_map/reduce_scatter | solution.py:92
Sparse Core Ops, SparseCore 0:
  11.1 23.2 reduce-scatter.5
  90.3 20.0 reduce-scatter.7
  127.7 19.3 reduce-scatter.9
  150.3 25.6 reduce-scatter.11
  179.0 25.7 reduce-scatter.13
where the time goes:
time: 212 us; the launch traced here: 211 us
  waiting for transfers between devices  99.1 us (47%)
  blocking collectives  57.2 us (27%)
  matrix products  24.2 us (11%)
  between operations  14.6 us (7%)
  other arithmetic  10.9 us (5%)
  local copies, waits for them, and re-layouts  5.01 us (2%)
    reduce_scatter x1, waiting for transfers between devices, per_device(): lax.psum_scatter(rounded(weight_part).astype(jnp.bfloat16), 'seq', scatte...  28.7 us
    reduce_scatter x1, waiting for transfers between devices, per_device(): lax.psum_scatter(rounded(query_part).astype(jnp.bfloat16), 'seq', scatter...  27.2 us
    reduce_scatter x1, waiting for transfers between devices, per_device(): lax.psum_scatter(jnp.dot(hidden, proj_weight, preferred_element_type=jnp....  22.6 us
    reduce_scatter x1, waiting for transfers between devices, per_device(): lax.psum_scatter((first + jnp.dot(value_grad, code_weight, preferred_elem...  20.2 us
    psum x2, blocking collectives, per_device(): lax.psum((jnp.sum(class_weight), jnp.sum(focal_value * class_weight[None,...  17.3 us
    all_gather x1, blocking collectives, per_device(): latent = lax.all_gather(latent_share, 'lab', axis=0, tiled=True)  14.8 us
    all_gather x1, blocking collectives, per_device(): pre_grad = lax.all_gather(pre_share_grad, 'lab', axis=0, tiled=True)  14.8 us
    psum x1, blocking collectives, per_device(): lax.psum(counts_local.astype(jnp.bfloat16), 'seq').astype(jnp.float32)  10.3 us
  transfers between devices with their start and end apart: 5, of which 5 were waited for; matrix products, arithmetic and copies ran while one was open for 6% of the time, Pallas kernels for 0%

commit v1 on v0

v1 whole, which is shorter than its diff:
```python
import functools
import math

import jax
import jax.numpy as jnp
from jax import lax
from jax.experimental import pallas as pl
from jax.experimental.pallas import tpu as pltpu
from jax.sharding import PartitionSpec as P

balance_beta = 0.9999
MESH = pl.DeviceIdType.MESH
F32 = jnp.float32
BF16 = jnp.bfloat16


def expm1(x):
    series = jnp.ones_like(x)
    for order in range(10, 1, -1):
        series = 1.0 + x * series * (1.0 / order)
    return jnp.where(jnp.abs(x) < 0.5, x * series, jnp.exp(x) - 1.0)


def nt(a, b):
    return lax.dot_general(a, b, (((1,), (1,)), ((), ())), preferred_element_type=F32)


def nn(a, b):
    return jnp.dot(a, b, preferred_element_type=F32)


def rows(start, size, multiple):
    return pl.ds(pl.multiple_of(start, multiple), size)


def tile_of(size):
    return 256 if size % 256 == 0 else size


def kernel(
    S, L, all_codes,
    hidden, proj, queries, codew, bias, labels, counts,
    loss_out, gh_out, gp_out, gq_out, gw_out, gb_out,
    pre_b, rs1, lat, latT, w_s, v_s, tot, cnt, sc, den_n, mean_n, grad_n,
    sg_s, vg_s, acc, lg_b, rs2, pg, pgT,
    pq, pw, pp, q1, w1, p1, qs, ws, ps, q2, w2, p2,
    cnt_sem, tot_sem, sc_sem, rs1_sem, ag1_sem, rs2_sem, ag2_sem, st1_sem, st2_sem,
):
    T, D = hidden.shape
    C, E = queries.shape
    notes = labels.shape[0]
    X = S // 2
    sh = T // L
    me_s = lax.axis_index("seq")
    me_l = lax.axis_index("lab")
    x = me_s // 2
    c = lax.rem(me_s, 2)
    lab_peers = [lax.rem(me_l + d, L) for d in range(1, L)]
    seq_peers = [lax.rem(me_s + d, S) for d in range(1, S)]
    sent = []

    def send(src, dst, sems, index, device):
        copy = pltpu.make_async_remote_copy(
            src_ref=src,
            dst_ref=dst,
            send_sem=sems.at[(0,) + index],
            recv_sem=sems.at[(1,) + index],
            device_id=device,
            device_id_type=MESH,
        )
        copy.start()
        sent.append(copy)
        return copy

    barrier = pltpu.get_barrier_semaphore()
    for peer in lab_peers:
        pl.semaphore_signal(barrier, inc=1, device_id={"lab": peer}, device_id_type=MESH)
    for peer in seq_peers:
        pl.semaphore_signal(barrier, inc=1, device_id={"seq": peer}, device_id_type=MESH)

    cnt[me_s] = counts[...].astype(F32)
    tr = tile_of(T)

    @pl.loop(0, T // tr)
    def _(i):
        at = rows(i * tr, tr, tr)
        pre_b[at, :] = nn(hidden[at, :], proj[...]).astype(BF16)

    pl.semaphore_wait(barrier, S + L - 2)

    def share(j):
        return rows(j * sh, sh, 16)

    copies = [
        send(pre_b.at[share(p)], rs1.at[d], rs1_sem, (d,), {"lab": p})
        for d, p in enumerate(lab_peers)
    ]
    cnt_copies = [
        send(cnt.at[me_s], cnt.at[me_s], cnt_sem, (d,), {"seq": p})
        for d, p in enumerate(seq_peers)
    ]
    total = pre_b[share(me_l), :].astype(F32)
    for d, copy in enumerate(copies):
        copy.wait_recv()
        total = total + rs1[d].astype(F32)
    lat[share(me_l), :] = jnp.tanh(total).astype(BF16)
    copies = [
        send(lat.at[share(me_l)], lat.at[share(me_l)], ag1_sem, (d,), {"lab": p})
        for d, p in enumerate(lab_peers)
    ]
    for copy in copies:
        copy.wait_recv()

    tc = tile_of(C)

    @pl.loop(0, C // tc)
    def _(i):
        at = rows(i * tc, tc, tc)
        weights = jnp.exp(nt(lat[...], queries[at, :]))
        values = nt(lat[...], codew[at, :])
        w_s[:, at] = weights
        v_s[:, at] = values
        tot[me_s, 0:1, at] = jnp.sum(weights, 0, keepdims=True)
        tot[me_s, 1:2, at] = jnp.sum(weights * values, 0, keepdims=True)

    copies = [
        send(tot.at[me_s], tot.at[me_s], tot_sem, (d,), {"seq": p})
        for d, p in enumerate(seq_peers)
    ]
    latT[...] = lat[...].astype(F32).T.astype(BF16)
    for copy in cnt_copies:
        copy.wait_recv()
    occurrences = jnp.ones((1, C), F32)
    for s in range(S):
        occurrences = occurrences + cnt[s]
    class_weight = (1.0 - balance_beta) / -expm1(occurrences * math.log(balance_beta))
    for copy in copies:
        copy.wait_recv()
    losses = []
    bias_grad = jnp.zeros((1, C), F32)
    for n in range(notes):
        both = jnp.zeros((2, C), F32)
        for s in range(S):
            if s * notes // S == n:
                both = both + tot[s]
        inverse = 1.0 / both[0:1, :]
        mean = both[1:2, :] / both[0:1, :]
        logit = mean + bias[...]
        y = labels[n : n + 1, :].astype(F32)
        t = jnp.exp(-jnp.abs(logit))
        l1p = jnp.log1p(t)
        big = 1.0 / (1.0 + t)
        small = t / (1.0 + t)
        p = jnp.where(logit >= 0, big, small)
        q = jnp.where(logit >= 0, small, big)
        ls_pos = jnp.minimum(logit, 0.0) - l1p
        ls_neg = jnp.minimum(-logit, 0.0) - l1p
        focal = -(y * q * q * ls_pos + (1.0 - y) * p * p * ls_neg)
        slope = -(
            y * q * q * (q - 2.0 * p * ls_pos)
            + (1.0 - y) * p * p * (2.0 * q * ls_neg - p)
        )
        grad = class_weight * slope
        bias_grad = bias_grad + grad
        den_n[n] = inverse
        mean_n[n] = mean
        grad_n[n] = grad
        losses.append(jnp.sum(focal * class_weight, 1, keepdims=True))
    sc[me_l] = jnp.concatenate(
        [
            jnp.broadcast_to(value, (1, 128))
            for value in [jnp.sum(class_weight, 1, keepdims=True)] + losses
        ],
        axis=0,
    )
    sc_copies = [
        send(sc.at[me_l], sc.at[me_l], sc_sem, (d,), {"lab": p})
        for d, p in enumerate(lab_peers)
    ]

    note = me_s * notes // S
    acc[...] = jnp.zeros_like(acc)

    @pl.loop(0, C // tc)
    def _(i):
        at = rows(i * tc, tc, tc)
        value_part = w_s[:, at] * den_n[note, :, at] * grad_n[note, :, at]
        score_part = value_part * (v_s[:, at] - mean_n[note, :, at])
        vg = value_part.astype(BF16)
        sg = score_part.astype(BF16)
        vg_s[:, at] = vg
        sg_s[:, at] = sg
        acc[...] += nn(sg, queries[at, :]) + nn(vg, codew[at, :])

    lg_b[...] = acc[...].astype(BF16)
    rs2_copies = [
        send(lg_b.at[share(p)], rs2.at[d], rs2_sem, (d,), {"lab": p})
        for d, p in enumerate(lab_peers)
    ]

    sister = {"seq": x * 2 + (1 - c)}
    slots = list(range(1, X)) + [0]
    xs = [lax.rem(x + d, X) for d in range(X)]

    def chunk(ref, k):
        size = ref.shape[0] // S
        return rows(k * size, size, 16)

    def stage1(a, part, first):
        out = {}
        for d in slots:
            k = xs[d] * 2 + (1 - c)
            out[d] = send(part.at[chunk(part, k)], first.at[d], st1_sem, (a, d), sister)
        return out

    def stage2(a, part, first, mid, second, arrived):
        out = []
        for d in range(1, X):
            arrived[d].wait_recv()
            mine = part[chunk(part, xs[d] * 2 + c), :].astype(F32)
            mid[d - 1] = (mine + first[d].astype(F32)).astype(BF16)
            out.append(
                send(
                    mid.at[d - 1], second.at[d - 1], st2_sem, (a, d - 1),
                    {"seq": xs[d] * 2 + c},
                )
            )
        return out

    def finish(part, first, second, arrived, copies, scale, out):
        arrived[0].wait_recv()
        total = part[chunk(part, me_s), :].astype(F32) + first[0].astype(F32)
        for d, copy in enumerate(copies):
            copy.wait_recv()
            total = total + second[d].astype(F32)
        out[...] = (total * scale).astype(BF16)

    def code_part(grads, part):
        @pl.loop(0, C // tc)
        def _(i):
            at = rows(i * tc, tc, tc)
            part[at, :] = nn(latT[...], grads[:, at]).T.astype(BF16)

    code_part(sg_s, pq)
    q_first = stage1(0, pq, q1)
    code_part(vg_s, pw)
    w_first = stage1(1, pw, w1)
    q_second = stage2(0, pq, q1, qs, q2, q_first)

    for copy in sc_copies:
        copy.wait_recv()
    scalars = sc[0]
    for j in range(1, L):
        scalars = scalars + sc[j]
    factor = all_codes / scalars[0:1, 0:1]
    loss_out[...] = scalars[1 : 1 + notes, :] * factor
    gb_out[...] = bias_grad * factor

    total = lg_b[share(me_l), :].astype(F32)
    for d, copy in enumerate(rs2_copies):
        copy.wait_recv()
        total = total + rs2[d].astype(F32)
    wide = lat[share(me_l), :].astype(F32)
    pg[share(me_l), :] = (total * factor * (1.0 - wide * wide)).astype(BF16)
    ag2_copies = [
        send(pg.at[share(me_l)], pg.at[share(me_l)], ag2_sem, (d,), {"lab": p})
        for d, p in enumerate(lab_peers)
    ]
    w_second = stage2(1, pw, w1, ws, w2, w_first)
    for copy in ag2_copies:
        copy.wait_recv()
    pgT[...] = pg[...].astype(F32).T.astype(BF16)
    td = tile_of(D)

    @pl.loop(0, D // td)
    def _(i):
        at = rows(i * td, td, td)
        pp[at, :] = nn(pgT[...], hidden[:, at]).T.astype(BF16)

    p_first = stage1(2, pp, p1)

    @pl.loop(0, D // td)
    def _(i):
        at = rows(i * td, td, td)
        gh_out[:, at] = nt(pg[...], proj[at, :]).astype(BF16)

    p_second = stage2(2, pp, p1, ps, p2, p_first)
    finish(pq, q1, q2, q_first, q_second, factor, gq_out)
    finish(pw, w1, w2, w_first, w_second, factor, gw_out)
    finish(pp, p1, p2, p_first, p_second, 1.0, gp_out)
    for copy in sent:
        copy.wait_send()


def per_device(hidden, proj_weight, queries, code_weight, code_bias, labels, code_counts):
    L = lax.axis_size("lab")
    S = lax.axis_size("seq")
    X = S // 2
    T, D = hidden.shape
    C, E = queries.shape
    notes = labels.shape[0]
    sh = T // L
    vmem = pltpu.VMEM
    dma = pltpu.SemaphoreType.DMA
    scratch = [
        vmem((T, E), BF16),
        vmem((L - 1, sh, E), BF16),
        vmem((T, E), BF16),
        vmem((E, T), BF16),
        vmem((T, C), F32),
        vmem((T, C), F32),
        vmem((S, 2, C), F32),
        vmem((S, 1, C), F32),
        vmem((L, 1 + notes, 128), F32),
        vmem((notes, 1, C), F32),
        vmem((notes, 1, C), F32),
        vmem((notes, 1, C), F32),
        vmem((T, C), BF16),
        vmem((T, C), BF16),
        vmem((T, E), F32),
        vmem((T, E), BF16),
        vmem((L - 1, sh, E), BF16),
        vmem((T, E), BF16),
        vmem((E, T), BF16),
        vmem((C, E), BF16),
        vmem((C, E), BF16),
        vmem((D, E), BF16),
        vmem((X, C // S, E), BF16),
        vmem((X, C // S, E), BF16),
        vmem((X, D // S, E), BF16),
        vmem((X - 1, C // S, E), BF16),
        vmem((X - 1, C // S, E), BF16),
        vmem((X - 1, D // S, E), BF16),
        vmem((X - 1, C // S, E), BF16),
        vmem((X - 1, C // S, E), BF16),
        vmem((X - 1, D // S, E), BF16),
        dma((2, S - 1)),
        dma((2, S - 1)),
        dma((2, L - 1)),
        dma((2, L - 1)),
        dma((2, L - 1)),
        dma((2, L - 1)),
        dma((2, L - 1)),
        dma((2, 3, X)),
        dma((2, 3, X - 1)),
    ]
    whole = pl.BlockSpec(memory_space=pltpu.VMEM)
    loss, gh, gp, gq, gw, gb = pl.pallas_call(
        functools.partial(kernel, S, L, float(C * L)),
        out_shape=(
            jax.ShapeDtypeStruct((notes, 128), F32),
            jax.ShapeDtypeStruct((T, D), BF16),
            jax.ShapeDtypeStruct((D // S, E), BF16),
            jax.ShapeDtypeStruct((C // S, E), BF16),
            jax.ShapeDtypeStruct((C // S, E), BF16),
            jax.ShapeDtypeStruct((1, C), F32),
        ),
        in_specs=[whole] * 7,
        out_specs=(whole,) * 6,
        scratch_shapes=scratch,
        compiler_params=pltpu.CompilerParams(
            collective_id=0, has_side_effects=True, vmem_limit_bytes=56 * 1024 * 1024
        ),
    )(
        hidden, proj_weight, queries, code_weight, code_bias.reshape(1, C), labels, code_counts
    )
    return loss[:, 0], gh, gp, gq, gw, gb.reshape(C)


def solution(mesh):
    placed = (
        P(("grp", "seq"), "lab"),
        P("lab", None),
        P("lab", None),
        P("lab", None),
        P("lab"),
        P("grp", "lab"),
        P(("grp", "seq"), "lab"),
    )
    return jax.shard_map(
        per_device,
        mesh=mesh,
        in_specs=placed,
        out_specs=(
            P("grp"),
            P(("grp", "seq"), "lab"),
            P(("grp", "lab", "seq"), None),
            P(("grp", "lab", "seq"), None),
            P(("grp", "lab", "seq"), None),
            P(("grp", "lab")),
        ),
        check_vma=False,
    )
```

time: 212 us -> 74.6 us (0.35)
  waiting for transfers between devices: 99.1 us -> 0 us
  Pallas kernels: 0 us -> 64.8 us
  blocking collectives: 57.2 us -> 0 us
  matrix products: 24.2 us -> 0 us
  between operations: 14.6 us -> 0.65 us
  other arithmetic: 10.9 us -> 1.33 us
  local copies, waits for them, and re-layouts: 5.01 us -> 7.45 us
    reduce_scatter x5 -> x0, waiting for transfers between devices: 99 us -> none  [the longest x1 28.7 us: per_device(): lax.psum_scatter(rounded(weight_part).astype(jnp.bfloat16), 'seq', scatte...]
    pallas_call x0 -> x1, Pallas kernels: none -> 64.8 us  [per_device(): pl.pallas_call(functools.partial(kernel, S, L, float(C * L)), out_shape=(...]
    all_gather x2 -> x0, blocking collectives: 29.6 us -> none  [the longest x1 14.8 us: per_device(): latent = lax.all_gather(latent_share, 'lab', axis=0, tiled=True)]
    psum x3 -> x0, blocking collectives: 27.6 us -> none  [the longest x2 17.3 us: per_device(): lax.psum((jnp.sum(class_weight), jnp.sum(focal_value * class_weight[None,...]
    dot_general x9 -> x0, matrix products: 24.2 us -> none  [the longest x1 4.78 us: per_device(): jnp.einsum('te,ce->tc', latent, code_weight, preferred_element_type=jnp.f...]
    convert_element_type x6 -> x0, other arithmetic: 8.72 us -> none  [the longest x1 6.04 us: per_device(): value_grad = value_part.astype(jnp.bfloat16)]
    unnamed x21 -> x10, local copies, waits for them, and re-layouts: 5.01 us -> 4.83 us
  transfers between devices with their start and end apart: 5 -> 0, of which waited for: 5 -> 0; matrix products, arithmetic and copies ran while one was open for 6% -> 0% of each run, Pallas kernels for 0% -> 0%
where the time goes in v1:
time: 74.6 us; the launch traced here: 74.2 us
  Pallas kernels  64.8 us (87%)
  local copies, waits for them, and re-layouts  7.45 us (10%)
  other arithmetic  1.33 us (2%)
    pallas_call x1, Pallas kernels, per_device(): pl.pallas_call(functools.partial(kernel, S, L, float(C * L)), out_shape=(...  64.8 us
    unnamed x10, local copies, waits for them, and re-layouts  4.83 us

profile of v1, /device:TPU:0, one launch (start us, length us, event | category | flops | bytes accessed | tf_op | source)
XLA Modules:
  0.0 74.2 jit_solution(9071205787653752647)
XLA Ops:
  0.6 1.3 %reshape.18.bias = f32[1,2304]{1,0:T(1,128)} reshape(f32[2304]{0:T(1024)} %param.11) | data formatting | bytes 18432 | tf_op jit(solution)/shard_map/reshape | solution.py:365
  1.9 64.8 %shard_map.118 = (f32[2,128]{1,0:T(2,128)}, bf16[768,1024]{1,0:T(8,128)(2,1)}, bf16[256,256]{1,0:T(8,128)(2,1)}, bf16[576,256]{1,0:T(8,128)(2,1)}, bf16[576,256]{1,0:T(8,128)(2,1)}, /*index=5*/f32[1,2304]{1,0:T(1,128)}) custom-call(bf16[768,1024]{1,0:T(8,128)(2,1)} %hidden.1, bf16[1024,256]{1,0:T(8,128)(2,1)} %proj.1, bf16[2304,256]{1,0:T(8,128)(2,1)} %queries.1, ...), custom_call_target="tpu_custom_call" | custom-call | tf_op jit(solution)/shard_map/pallas_call | solution.py:348
  66.8 1.3 %slice_reduce_fusion = f32[2]{0:T(128)} fusion(f32[2,128]{1,0:T(2,128)} %get-tuple-element.12), kind=kLoop, calls=%fused_computation | loop fusion | bytes 16 | tf_op jit(solution)/shard_map/slice | solution.py:367
  68.1 1.3 %reduce.1 = f32[2304]{0:T(1024)} reduce(f32[1,2304]{1,0:T(1,128)} %get-tuple-element.17, f32[]{:T(128)} %constant.1), dimensions={0}, to_apply=%get-tuple-element.17.reduce_sub_computation | reduce | bytes 18436 | tf_op jit(solution)/shard_map/pallas_call | solution.py:348
  69.4 0.0 copy-start.2
  69.4 0.0 copy-start.1
  69.4 0.0 copy-start
  69.4 2.7 %copy.17 = bf16[768,1024]{1,0:T(8,128)(2,1)} copy(bf16[768,1024]{1,0:T(8,128)(2,1)} %get-tuple-element.25) | data formatting | bytes 3145728
  72.2 0.0 copy-done.2
  72.2 0.7 copy.18
  72.8 0.0 copy-done.1
  72.8 0.7 copy.19
  73.5 0.0 copy-done
  73.5 0.7 copy.20
Async XLA Ops:
  69.4 2.7 %copy-start.2 = (bf16[256,256]{1,0:T(8,128)(2,1)S(1)}, bf16[256,256]{1,0:T(8,128)(2,1)}, u32[]{:S(2)}) copy-start(bf16[256,256]{1,0:T(8,128)(2,1)} %get-tuple-element.26) | copy-start | bytes 393220
  69.4 3.4 %copy-start.1 = (bf16[576,256]{1,0:T(8,128)(2,1)S(1)}, bf16[576,256]{1,0:T(8,128)(2,1)}, u32[]{:S(2)}) copy-start(bf16[576,256]{1,0:T(8,128)(2,1)} %get-tuple-element.27) | copy-start | bytes 884740
  69.4 4.1 %copy-start = (bf16[576,256]{1,0:T(8,128)(2,1)S(1)}, bf16[576,256]{1,0:T(8,128)(2,1)}, u32[]{:S(2)}) copy-start(bf16[576,256]{1,0:T(8,128)(2,1)} %get-tuple-element.28) | copy-start | bytes 884740

commit v2 on v1

--- a/solution.py
+++ b/solution.py
@@ -33,15 +33,22 @@
     return pl.ds(pl.multiple_of(start, multiple), size)
 
 
-def tile_of(size):
-    return 256 if size % 256 == 0 else size
+def tile_of(size, most=768):
+    for tile in (768, 512, 256):
+        if tile <= most and size % tile == 0:
+            return tile
+    return size
+
+
+def far_first(count):
+    return sorted(range(1, count), key=lambda d: -min(d, count - d))
 
 
 def kernel(
     S, L, all_codes,
-    hidden, proj, queries, codew, bias, labels, counts,
-    loss_out, gh_out, gp_out, gq_out, gw_out, gb_out,
-    pre_b, rs1, lat, latT, w_s, v_s, tot, cnt, sc, den_n, mean_n, grad_n,
+    hidden_h, proj_h, queries_h, codew_h, bias, labels, counts,
+    loss_out, pg_out, gp_out, gq_out, gw_out, gb_out,
+    hidden, proj, queries, codew, load_sem, pre_b, rs1, lat, latT, w_s, v_s, tot, cnt, sc, den_n, mean_n, grad_n,
     sg_s, vg_s, acc, lg_b, rs2, pg, pgT,
     pq, pw, pp, q1, w1, p1, qs, ws, ps, q2, w2, p2,
     cnt_sem, tot_sem, sc_sem, rs1_sem, ag1_sem, rs2_sem, ag2_sem, st1_sem, st2_sem,
@@ -78,50 +85,71 @@
     for peer in seq_peers:
         pl.semaphore_signal(barrier, inc=1, device_id={"seq": peer}, device_id_type=MESH)
 
+    loads = [
+        pltpu.make_async_copy(src, dst, load_sem.at[k])
+        for k, (src, dst) in enumerate(
+            [(proj_h, proj), (hidden_h, hidden), (queries_h, queries), (codew_h, codew)]
+        )
+    ]
+    for load in loads:
+        load.start()
     cnt[me_s] = counts[...].astype(F32)
-    tr = tile_of(T)
-
-    @pl.loop(0, T // tr)
-    def _(i):
-        at = rows(i * tr, tr, tr)
-        pre_b[at, :] = nn(hidden[at, :], proj[...]).astype(BF16)
-
-    pl.semaphore_wait(barrier, S + L - 2)
+    loads[0].wait()
+    loads[1].wait()
 
     def share(j):
         return rows(j * sh, sh, 16)
 
-    copies = [
-        send(pre_b.at[share(p)], rs1.at[d], rs1_sem, (d,), {"lab": p})
-        for d, p in enumerate(lab_peers)
-    ]
+    def project(j):
+        pre_b[share(j), :] = nn(hidden[share(j), :], proj[...]).astype(BF16)
+
+    lab_order = far_first(L)
+    copies = {}
+    for k, d in enumerate(lab_order):
+        p = lab_peers[d - 1]
+        project(p)
+        if k == 0:
+            pl.semaphore_wait(barrier, S + L - 2)
+        copies[d] = send(pre_b.at[share(p)], rs1.at[d - 1], rs1_sem, (d - 1,), {"lab": p})
+    project(me_l)
     cnt_copies = [
         send(cnt.at[me_s], cnt.at[me_s], cnt_sem, (d,), {"seq": p})
         for d, p in enumerate(seq_peers)
     ]
     total = pre_b[share(me_l), :].astype(F32)
-    for d, copy in enumerate(copies):
-        copy.wait_recv()
-        total = total + rs1[d].astype(F32)
+    for d in reversed(lab_order):
+        copies[d].wait_recv()
+        total = total + rs1[d - 1].astype(F32)
     lat[share(me_l), :] = jnp.tanh(total).astype(BF16)
-    copies = [
-        send(lat.at[share(me_l)], lat.at[share(me_l)], ag1_sem, (d,), {"lab": p})
-        for d, p in enumerate(lab_peers)
-    ]
-    for copy in copies:
-        copy.wait_recv()
+    copies = {
+        d: send(
+            lat.at[share(me_l)], lat.at[share(me_l)], ag1_sem, (d - 1,), {"lab": lab_peers[d - 1]}
+        )
+        for d in lab_order
+    }
+    loads[2].wait()
+    loads[3].wait()
 
     tc = tile_of(C)
-
-    @pl.loop(0, C // tc)
-    def _(i):
-        at = rows(i * tc, tc, tc)
-        weights = jnp.exp(nt(lat[...], queries[at, :]))
-        values = nt(lat[...], codew[at, :])
-        w_s[:, at] = weights
-        v_s[:, at] = values
-        tot[me_s, 0:1, at] = jnp.sum(weights, 0, keepdims=True)
-        tot[me_s, 1:2, at] = jnp.sum(weights * values, 0, keepdims=True)
+    tot[me_s] = jnp.zeros((2, C), F32)
+
+    def attend(j):
+        block = lat[share(j), :]
+
+        @pl.loop(0, C // tc)
+        def _(i):
+            at = rows(i * tc, tc, tc)
+            weights = jnp.exp(nt(block, queries[at, :]))
+            values = nt(block, codew[at, :])
+            w_s[share(j), at] = weights
+            v_s[share(j), at] = values
+            tot[me_s, 0:1, at] += jnp.sum(weights, 0, keepdims=True)
+            tot[me_s, 1:2, at] += jnp.sum(weights * values, 0, keepdims=True)
+
+    attend(me_l)
+    for d in reversed(lab_order):
+        copies[d].wait_recv()
+        attend(lax.rem(me_l + L - d, L))
 
     copies = [
         send(tot.at[me_s], tot.at[me_s], tot_sem, (d,), {"seq": p})
@@ -145,7 +173,7 @@
                 both = both + tot[s]
         inverse = 1.0 / both[0:1, :]
         mean = both[1:2, :] / both[0:1, :]
-        logit = mean + bias[...]
+        logit = mean + bias[...][None, :]
         y = labels[n : n + 1, :].astype(F32)
         t = jnp.exp(-jnp.abs(logit))
         l1p = jnp.log1p(t)
@@ -179,25 +207,6 @@
     ]
 
     note = me_s * notes // S
-    acc[...] = jnp.zeros_like(acc)
-
-    @pl.loop(0, C // tc)
-    def _(i):
-        at = rows(i * tc, tc, tc)
-        value_part = w_s[:, at] * den_n[note, :, at] * grad_n[note, :, at]
-        score_part = value_part * (v_s[:, at] - mean_n[note, :, at])
-        vg = value_part.astype(BF16)
-        sg = score_part.astype(BF16)
-        vg_s[:, at] = vg
-        sg_s[:, at] = sg
-        acc[...] += nn(sg, queries[at, :]) + nn(vg, codew[at, :])
-
-    lg_b[...] = acc[...].astype(BF16)
-    rs2_copies = [
-        send(lg_b.at[share(p)], rs2.at[d], rs2_sem, (d,), {"lab": p})
-        for d, p in enumerate(lab_peers)
-    ]
-
     sister = {"seq": x * 2 + (1 - c)}
     slots = list(range(1, X)) + [0]
     xs = [lax.rem(x + d, X) for d in range(X)]
@@ -235,17 +244,48 @@
             total = total + second[d].astype(F32)
         out[...] = (total * scale).astype(BF16)
 
+    tw = tile_of(C, 256)
+
     def code_part(grads, part):
+        @pl.loop(0, C // tw)
+        def _(i):
+            at = rows(i * tw, tw, tw)
+            part[at, :] = nn(latT[...], grads[:, at]).T.astype(BF16)
+
+    @pl.loop(0, C // tw)
+    def _(i):
+        at = rows(i * tw, tw, tw)
+        value_part = w_s[:, at] * den_n[note, :, at] * grad_n[note, :, at]
+        vg = value_part.astype(BF16)
+        w_s[:, at] = value_part
+        vg_s[:, at] = vg
+        pw[at, :] = nn(latT[...], vg).T.astype(BF16)
+
+    w_first = stage1(1, pw, w1)
+
+    def latent_grad(j):
+        acc[...] = jnp.zeros_like(acc)
+
         @pl.loop(0, C // tc)
         def _(i):
             at = rows(i * tc, tc, tc)
-            part[at, :] = nn(latT[...], grads[:, at]).T.astype(BF16)
-
+            score_part = w_s[share(j), at] * (v_s[share(j), at] - mean_n[note, :, at])
+            sg = score_part.astype(BF16)
+            sg_s[share(j), at] = sg
+            acc[...] += nn(sg, queries[at, :]) + nn(vg_s[share(j), at], codew[at, :])
+
+    rs2_copies = {}
+    w_second = None
+    for k, d in enumerate(lab_order):
+        p = lab_peers[d - 1]
+        latent_grad(p)
+        lg_b[share(p), :] = acc[...].astype(BF16)
+        rs2_copies[d] = send(lg_b.at[share(p)], rs2.at[d - 1], rs2_sem, (d - 1,), {"lab": p})
+        if k == 0:
+            w_second = stage2(1, pw, w1, ws, w2, w_first)
+    latent_grad(me_l)
     code_part(sg_s, pq)
     q_first = stage1(0, pq, q1)
-    code_part(vg_s, pw)
-    w_first = stage1(1, pw, w1)
-    q_second = stage2(0, pq, q1, qs, q2, q_first)
 
     for copy in sc_copies:
         copy.wait_recv()
@@ -256,21 +296,21 @@
     loss_out[...] = scalars[1 : 1 + notes, :] * factor
     gb_out[...] = bias_grad * factor
 
-    total = lg_b[share(me_l), :].astype(F32)
-    for d, copy in enumerate(rs2_copies):
-        copy.wait_recv()
-        total = total + rs2[d].astype(F32)
+    total = acc[...]
+    for d in reversed(lab_order):
+        rs2_copies[d].wait_recv()
+        total = total + rs2[d - 1].astype(F32)
     wide = lat[share(me_l), :].astype(F32)
     pg[share(me_l), :] = (total * factor * (1.0 - wide * wide)).astype(BF16)
     ag2_copies = [
         send(pg.at[share(me_l)], pg.at[share(me_l)], ag2_sem, (d,), {"lab": p})
         for d, p in enumerate(lab_peers)
     ]
-    w_second = stage2(1, pw, w1, ws, w2, w_first)
+    q_second = stage2(0, pq, q1, qs, q2, q_first)
     for copy in ag2_copies:
         copy.wait_recv()
     pgT[...] = pg[...].astype(F32).T.astype(BF16)
-    td = tile_of(D)
+    td = tile_of(D, 256)
 
     @pl.loop(0, D // td)
     def _(i):
@@ -279,17 +319,33 @@
 
     p_first = stage1(2, pp, p1)
 
-    @pl.loop(0, D // td)
-    def _(i):
-        at = rows(i * td, td, td)
-        gh_out[:, at] = nt(pg[...], proj[at, :]).astype(BF16)
-
+    pg_out[...] = pg[...]
     p_second = stage2(2, pp, p1, ps, p2, p_first)
+    finish(pw, w1, w2, w_first, w_second, factor, gw_out)
     finish(pq, q1, q2, q_first, q_second, factor, gq_out)
-    finish(pw, w1, w2, w_first, w_second, factor, gw_out)
     finish(pp, p1, p2, p_first, p_second, 1.0, gp_out)
     for copy in sent:
         copy.wait_send()
+
+
+def finish_kernel(
+    loss, pg, gp, gq, gw, gb, proj, loss_out, gh_out, gp_out, gq_out, gw_out, gb_out, gh, sem
+):
+    copies = []
+    for k, (src, dst) in enumerate([(gp, gp_out), (gq, gq_out), (gw, gw_out)]):
+        copies.append(pltpu.make_async_copy(src, dst, sem.at[k]))
+        copies[-1].start()
+    part = gh.shape[0] // 4
+    for k in range(4):
+        at = pl.ds(k * part, part)
+        gh[at, :] = nt(pg[at, :], proj[...]).astype(BF16)
+        copies.append(pltpu.make_async_copy(gh.at[at], gh_out.at[at], sem.at[3 + k]))
+        copies[-1].start()
+    gb_out[...] = gb[0, :]
+    for n in range(loss_out.shape[0]):
+        loss_out[n] = jnp.max(loss[n : n + 1, :])
+    for copy in copies:
+        copy.wait()
 
 
 def per_device(hidden, proj_weight, queries, code_weight, code_bias, labels, code_counts):
@@ -303,6 +359,11 @@
     vmem = pltpu.VMEM
     dma = pltpu.SemaphoreType.DMA
     scratch = [
+        vmem((T, D), BF16),
+        vmem((D, E), BF16),
+        vmem((C, E), BF16),
+        vmem((C, E), BF16),
+        dma((4,)),
         vmem((T, E), BF16),
         vmem((L - 1, sh, E), BF16),
         vmem((T, E), BF16),
@@ -317,7 +378,7 @@
         vmem((notes, 1, C), F32),
         vmem((T, C), BF16),
         vmem((T, C), BF16),
-        vmem((T, E), F32),
+        vmem((sh, E), F32),
         vmem((T, E), BF16),
         vmem((L - 1, sh, E), BF16),
         vmem((T, E), BF16),
@@ -345,26 +406,46 @@
         dma((2, 3, X - 1)),
     ]
     whole = pl.BlockSpec(memory_space=pltpu.VMEM)
-    loss, gh, gp, gq, gw, gb = pl.pallas_call(
+    anywhere = pl.BlockSpec(memory_space=pl.ANY)
+    shapes = dict(
+        gp=jax.ShapeDtypeStruct((D // S, E), BF16),
+        gq=jax.ShapeDtypeStruct((C // S, E), BF16),
+        gw=jax.ShapeDtypeStruct((C // S, E), BF16),
+    )
+    loss, pg, gp, gq, gw, gb = pl.pallas_call(
         functools.partial(kernel, S, L, float(C * L)),
         out_shape=(
             jax.ShapeDtypeStruct((notes, 128), F32),
-            jax.ShapeDtypeStruct((T, D), BF16),
-            jax.ShapeDtypeStruct((D // S, E), BF16),
-            jax.ShapeDtypeStruct((C // S, E), BF16),
-            jax.ShapeDtypeStruct((C // S, E), BF16),
+            jax.ShapeDtypeStruct((T, E), BF16),
+            *shapes.values(),
             jax.ShapeDtypeStruct((1, C), F32),
         ),
-        in_specs=[whole] * 7,
+        in_specs=[anywhere] * 4 + [whole] * 3,
         out_specs=(whole,) * 6,
         scratch_shapes=scratch,
         compiler_params=pltpu.CompilerParams(
             collective_id=0, has_side_effects=True, vmem_limit_bytes=56 * 1024 * 1024
         ),
-    )(
-        hidden, proj_weight, queries, code_weight, code_bias.reshape(1, C), labels, code_counts
-    )
-    return loss[:, 0], gh, gp, gq, gw, gb.reshape(C)
+    )(hidden, proj_weight, queries, code_weight, code_bias, labels, code_counts)
+    return pl.pallas_call(
+        finish_kernel,
+        out_shape=(
+            jax.ShapeDtypeStruct((notes,), F32),
+            jax.ShapeDtypeStruct((T, D), BF16),
+            *shapes.values(),
+            jax.ShapeDtypeStruct((C,), F32),
+        ),
+        in_specs=[whole] * 7,
+        out_specs=(
+            pl.BlockSpec(memory_space=pltpu.SMEM),
+            anywhere,
+            anywhere,
+            anywhere,
+            anywhere,
+            whole,
+        ),
+        scratch_shapes=[vmem((T, D), BF16), dma((7,))],
+    )(loss, pg, gp, gq, gw, gb, proj_weight)
 
 
 def solution(mesh):

time: 74.6 us -> 66.9 us (0.90)
  local copies, waits for them, and re-layouts: 7.45 us -> 0 us
  other arithmetic: 1.33 us -> 0 us
  Pallas kernels: 64.8 us -> 66 us
    unnamed x10 -> x0, local copies, waits for them, and re-layouts: 4.83 us -> none
    pallas_call x0 -> x1, Pallas kernels: none -> 3.66 us  [per_device(): pl.pallas_call(finish_kernel, out_shape=(jax.ShapeDtypeStruct((notes,), F...]
    pallas_call x1, Pallas kernels: 64.8 us -> 62.4 us  [per_device(): pl.pallas_call(functools.partial(kernel, S, L, float(C * L)), out_shape=(...]
    pallas_call x1 -> x0, other arithmetic: 1.33 us -> none  [per_device(): pl.pallas_call(functools.partial(kernel, S, L, float(C * L)), out_shape=(...]
    reshape x1 -> x0, local copies, waits for them, and re-layouts: 1.31 us -> none  [per_device(): code_bias.reshape(1, C)]
    slice x1 -> x0, local copies, waits for them, and re-layouts: 1.31 us -> none  [per_device(): return (loss[:, 0], gh, gp, gq, gw, gb.reshape(C))]
where the time goes in v2:
time: 66.9 us; the launch traced here: 66.7 us
  Pallas kernels  66 us (99%)
    pallas_call x1, Pallas kernels, per_device(): pl.pallas_call(functools.partial(kernel, S, L, float(C * L)), out_shape=(...  62.4 us
    pallas_call x1, Pallas kernels, per_device(): pl.pallas_call(finish_kernel, out_shape=(jax.ShapeDtypeStruct((notes,), F...  3.66 us

profile of v2, /device:TPU:0, one launch (start us, length us, event | category | flops | bytes accessed | tf_op | source)
XLA Modules:
  0.0 66.7 jit_solution(7446460376855429689)
XLA Ops:
  0.6 62.4 %shard_map.118 = (f32[2,128]{1,0:T(2,128)}, bf16[768,256]{1,0:T(8,128)(2,1)}, bf16[256,256]{1,0:T(8,128)(2,1)}, bf16[576,256]{1,0:T(8,128)(2,1)}, bf16[576,256]{1,0:T(8,128)(2,1)}, /*index=5*/f32[1,2304]{1,0:T(1,128)}) custom-call(bf16[768,1024]{1,0:T(8,128)(2,1)} %hidden_h.1, bf16[1024,256]{1,0:T(8,128)(2,1)} %proj.1, bf16[2304,256]{1,0:T(8,128)(2,1)} %queries_h.1, ...), custom_call_target="tpu_custom_call" | custom-call | tf_op jit(solution)/shard_map/pallas_call | solution.py:415
  63.0 3.7 %shard_map.119 = (f32[2]{0:T(128)}, bf16[768,1024]{1,0:T(8,128)(2,1)}, bf16[256,256]{1,0:T(8,128)(2,1)}, bf16[576,256]{1,0:T(8,128)(2,1)}, bf16[576,256]{1,0:T(8,128)(2,1)}, /*index=5*/f32[2304]{0:T(1024)}) custom-call(f32[2,128]{1,0:T(2,128)} %get-tuple-element.12.loss, bf16[768,256]{1,0:T(8,128)(2,1)} %get-tuple-element.13.pg, ...), custom_call_target="tpu_custom_call" | custom-call | tf_op jit(solution)/shard_map/pallas_call | solution.py:430

commit v3 on v2

--- a/solution.py
+++ b/solution.py
@@ -65,6 +65,7 @@
     lab_peers = [lax.rem(me_l + d, L) for d in range(1, L)]
     seq_peers = [lax.rem(me_s + d, S) for d in range(1, S)]
     sent = []
+    sent_if = []
 
     def send(src, dst, sems, index, device):
         copy = pltpu.make_async_remote_copy(
@@ -79,6 +80,51 @@
         sent.append(copy)
         return copy
 
+    line = L == 4
+    gather_order = [2, 1, 3] if line else list(reversed(far_first(L)))
+
+    def share(j):
+        return rows(j * (T // L), T // L, 16)
+
+    def gather_start(ref, sems):
+        out = {}
+        for d in [2, 1, 3] if line else far_first(L):
+            mine = ref.at[share(me_l)]
+            copy = pltpu.make_async_remote_copy(
+                src_ref=mine,
+                dst_ref=mine,
+                send_sem=sems.at[0, d - 1],
+                recv_sem=sems.at[1, d - 1],
+                device_id={"lab": lab_peers[d - 1]},
+                device_id_type=MESH,
+            )
+            if line and d != 2:
+                near = me_l != (3 if d == 1 else 0)
+                pl.when(near)(copy.start)
+                sent_if.append((near, copy))
+            else:
+                copy.start()
+                sent.append(copy)
+            out[d] = copy
+        return out
+
+    def relay(ref, sems):
+        if not line:
+            return
+        inner = jnp.logical_or(me_l == 1, me_l == 2)
+        block = ref.at[share(lax.rem(me_l + 2, L))]
+        end = lax.rem(3 * (me_l + 3), 4)
+        copy = pltpu.make_async_remote_copy(
+            src_ref=block,
+            dst_ref=block,
+            send_sem=sems.at[0, L - 1],
+            recv_sem=sems.at[1, end * 2 // 3],
+            device_id={"lab": end},
+            device_id_type=MESH,
+        )
+        pl.when(inner)(copy.start)
+        sent_if.append((inner, copy))
+
     barrier = pltpu.get_barrier_semaphore()
     for peer in lab_peers:
         pl.semaphore_signal(barrier, inc=1, device_id={"lab": peer}, device_id_type=MESH)
@@ -96,9 +142,6 @@
     cnt[me_s] = counts[...].astype(F32)
     loads[0].wait()
     loads[1].wait()
-
-    def share(j):
-        return rows(j * sh, sh, 16)
 
     def project(j):
         pre_b[share(j), :] = nn(hidden[share(j), :], proj[...]).astype(BF16)
@@ -121,12 +164,7 @@
         copies[d].wait_recv()
         total = total + rs1[d - 1].astype(F32)
     lat[share(me_l), :] = jnp.tanh(total).astype(BF16)
-    copies = {
-        d: send(
-            lat.at[share(me_l)], lat.at[share(me_l)], ag1_sem, (d - 1,), {"lab": lab_peers[d - 1]}
-        )
-        for d in lab_order
-    }
+    copies = gather_start(lat, ag1_sem)
     loads[2].wait()
     loads[3].wait()
 
@@ -147,8 +185,10 @@
             tot[me_s, 1:2, at] += jnp.sum(weights * values, 0, keepdims=True)
 
     attend(me_l)
-    for d in reversed(lab_order):
+    for d in gather_order:
         copies[d].wait_recv()
+        if d == 2:
+            relay(lat, ag1_sem)
         attend(lax.rem(me_l + L - d, L))
 
     copies = [
@@ -252,40 +292,32 @@
             at = rows(i * tw, tw, tw)
             part[at, :] = nn(latT[...], grads[:, at]).T.astype(BF16)
 
-    @pl.loop(0, C // tw)
-    def _(i):
-        at = rows(i * tw, tw, tw)
-        value_part = w_s[:, at] * den_n[note, :, at] * grad_n[note, :, at]
-        vg = value_part.astype(BF16)
-        w_s[:, at] = value_part
-        vg_s[:, at] = vg
-        pw[at, :] = nn(latT[...], vg).T.astype(BF16)
-
-    w_first = stage1(1, pw, w1)
-
     def latent_grad(j):
         acc[...] = jnp.zeros_like(acc)
 
         @pl.loop(0, C // tc)
         def _(i):
             at = rows(i * tc, tc, tc)
-            score_part = w_s[share(j), at] * (v_s[share(j), at] - mean_n[note, :, at])
+            value_part = w_s[share(j), at] * den_n[note, :, at] * grad_n[note, :, at]
+            score_part = value_part * (v_s[share(j), at] - mean_n[note, :, at])
+            vg = value_part.astype(BF16)
             sg = score_part.astype(BF16)
+            vg_s[share(j), at] = vg
             sg_s[share(j), at] = sg
-            acc[...] += nn(sg, queries[at, :]) + nn(vg_s[share(j), at], codew[at, :])
+            acc[...] += nn(sg, queries[at, :]) + nn(vg, codew[at, :])
 
     rs2_copies = {}
-    w_second = None
-    for k, d in enumerate(lab_order):
+    for d in lab_order:
         p = lab_peers[d - 1]
         latent_grad(p)
         lg_b[share(p), :] = acc[...].astype(BF16)
         rs2_copies[d] = send(lg_b.at[share(p)], rs2.at[d - 1], rs2_sem, (d - 1,), {"lab": p})
-        if k == 0:
-            w_second = stage2(1, pw, w1, ws, w2, w_first)
     latent_grad(me_l)
+    code_part(vg_s, pw)
+    w_first = stage1(1, pw, w1)
     code_part(sg_s, pq)
     q_first = stage1(0, pq, q1)
+    w_second = stage2(1, pw, w1, ws, w2, w_first)
 
     for copy in sc_copies:
         copy.wait_recv()
@@ -302,13 +334,12 @@
         total = total + rs2[d - 1].astype(F32)
     wide = lat[share(me_l), :].astype(F32)
     pg[share(me_l), :] = (total * factor * (1.0 - wide * wide)).astype(BF16)
-    ag2_copies = [
-        send(pg.at[share(me_l)], pg.at[share(me_l)], ag2_sem, (d,), {"lab": p})
-        for d, p in enumerate(lab_peers)
-    ]
+    ag2_copies = gather_start(pg, ag2_sem)
     q_second = stage2(0, pq, q1, qs, q2, q_first)
-    for copy in ag2_copies:
-        copy.wait_recv()
+    for d in gather_order:
+        ag2_copies[d].wait_recv()
+        if d == 2:
+            relay(pg, ag2_sem)
     pgT[...] = pg[...].astype(F32).T.astype(BF16)
     td = tile_of(D, 256)
 
@@ -326,6 +357,8 @@
     finish(pp, p1, p2, p_first, p_second, 1.0, gp_out)
     for copy in sent:
         copy.wait_send()
+    for started, copy in sent_if:
+        pl.when(started)(copy.wait_send)
 
 
 def finish_kernel(
@@ -399,9 +432,9 @@
         dma((2, S - 1)),
         dma((2, L - 1)),
         dma((2, L - 1)),
+        dma((2, L)),
         dma((2, L - 1)),
-        dma((2, L - 1)),
-        dma((2, L - 1)),
+        dma((2, L)),
         dma((2, 3, X)),
         dma((2, 3, X - 1)),
     ]

time: 66.9 us -> 62.5 us (0.934)
  Pallas kernels: 66 us -> 61.7 us
    pallas_call x1, Pallas kernels: 62.4 us -> 58 us  [per_device(): pl.pallas_call(functools.partial(kernel, S, L, float(C * L)), out_shape=(...]
where the time goes in v3:
time: 62.5 us; the launch traced here: 62.3 us
  Pallas kernels  61.7 us (99%)
  between operations  0.64 us (1%)
    pallas_call x1, Pallas kernels, per_device(): pl.pallas_call(functools.partial(kernel, S, L, float(C * L)), out_shape=(...  58 us
    pallas_call x1, Pallas kernels, per_device(): pl.pallas_call(finish_kernel, out_shape=(jax.ShapeDtypeStruct((notes,), F...  3.66 us

profile of v3, /device:TPU:0, one launch (start us, length us, event | category | flops | bytes accessed | tf_op | source)
XLA Modules:
  0.0 62.3 jit_solution(722370100069337160)
XLA Ops:
  0.6 58.0 %shard_map.118 = (f32[2,128]{1,0:T(2,128)}, bf16[768,256]{1,0:T(8,128)(2,1)}, bf16[256,256]{1,0:T(8,128)(2,1)}, bf16[576,256]{1,0:T(8,128)(2,1)}, bf16[576,256]{1,0:T(8,128)(2,1)}, /*index=5*/f32[1,2304]{1,0:T(1,128)}) custom-call(bf16[768,1024]{1,0:T(8,128)(2,1)} %hidden_h.1, bf16[1024,256]{1,0:T(8,128)(2,1)} %proj.1, bf16[2304,256]{1,0:T(8,128)(2,1)} %queries_h.1, ...), custom_call_target="tpu_custom_call" | custom-call | tf_op jit(solution)/shard_map/pallas_call | solution.py:448
  58.6 3.7 %shard_map.119 = (f32[2]{0:T(128)}, bf16[768,1024]{1,0:T(8,128)(2,1)}, bf16[256,256]{1,0:T(8,128)(2,1)}, bf16[576,256]{1,0:T(8,128)(2,1)}, bf16[576,256]{1,0:T(8,128)(2,1)}, /*index=5*/f32[2304]{0:T(1024)}) custom-call(f32[2,128]{1,0:T(2,128)} %get-tuple-element.12.loss, bf16[768,256]{1,0:T(8,128)(2,1)} %get-tuple-element.13.pg, ...), custom_call_target="tpu_custom_call" | custom-call | tf_op jit(solution)/shard_map/pallas_call | solution.py:463

commit v4 on v3

--- a/solution.py
+++ b/solution.py
@@ -111,7 +111,6 @@
     def relay(ref, sems):
         if not line:
             return
-        inner = jnp.logical_or(me_l == 1, me_l == 2)
         block = ref.at[share(lax.rem(me_l + 2, L))]
         end = lax.rem(3 * (me_l + 3), 4)
         copy = pltpu.make_async_remote_copy(
@@ -125,6 +124,71 @@
         pl.when(inner)(copy.start)
         sent_if.append((inner, copy))
 
+    reduce_order = [3, 1, 2] if line else far_first(L)
+    inner = jnp.logical_or(me_l == 1, me_l == 2)
+    outer = jnp.logical_or(me_l == 0, me_l == L - 1)
+
+    def arrive(slots, sems, k):
+        pltpu.make_async_remote_copy(
+            src_ref=slots.at[k],
+            dst_ref=slots.at[k],
+            send_sem=sems.at[0, k],
+            recv_sem=sems.at[1, k],
+            device_id={"lab": lab_peers[0]},
+            device_id_type=MESH,
+        ).wait_recv()
+
+    def term_copy(ref, slots, sems, d):
+        device, slot = lab_peers[d - 1], d - 1
+        if line and d != 2:
+            far = me_l // 3 if d == 1 else (3 - me_l) // 3
+            device = device * (1 - far) + (2 if d == 1 else 1) * far
+            slot = 3 * far if d == 1 else 2 + far
+        return pltpu.make_async_remote_copy(
+            src_ref=ref.at[share(lab_peers[d - 1])],
+            dst_ref=slots.at[slot],
+            send_sem=sems.at[0, d - 1],
+            recv_sem=sems.at[1, slot],
+            device_id={"lab": device},
+            device_id_type=MESH,
+        )
+
+    def term_send(ref, slots, sems, d):
+        copy = term_copy(ref, slots, sems, d)
+        if line and d == 2:
+            pl.when(outer)(copy.start)
+        else:
+            copy.start()
+        sent.append(copy)
+
+    def term_join(ref, slots, sems):
+        if not line:
+            return
+
+        @pl.when(inner)
+        def _():
+            arrive(slots, sems, 3)
+            at = share(lab_peers[1])
+            ref[at, :] = (ref[at, :].astype(F32) + slots[3].astype(F32)).astype(BF16)
+            term_copy(ref, slots, sems, 2).start()
+
+    def term_sum(total, slots, sems):
+        for d in [1, 3, 2] if line else reversed(reduce_order):
+            if line and d != 2:
+                absent = me_l == (0 if d == 1 else 3)
+
+                @pl.when(absent)
+                def _():
+                    slots[d - 1] = jnp.zeros_like(slots[d - 1])
+
+                @pl.when(jnp.logical_not(absent))
+                def _():
+                    arrive(slots, sems, d - 1)
+            else:
+                arrive(slots, sems, d - 1)
+            total = total + slots[d - 1].astype(F32)
+        return total
+
     barrier = pltpu.get_barrier_semaphore()
     for peer in lab_peers:
         pl.semaphore_signal(barrier, inc=1, device_id={"lab": peer}, device_id_type=MESH)
@@ -146,23 +210,19 @@
     def project(j):
         pre_b[share(j), :] = nn(hidden[share(j), :], proj[...]).astype(BF16)
 
-    lab_order = far_first(L)
-    copies = {}
-    for k, d in enumerate(lab_order):
+    for k, d in enumerate(reduce_order):
         p = lab_peers[d - 1]
         project(p)
         if k == 0:
             pl.semaphore_wait(barrier, S + L - 2)
-        copies[d] = send(pre_b.at[share(p)], rs1.at[d - 1], rs1_sem, (d - 1,), {"lab": p})
+        term_send(pre_b, rs1, rs1_sem, d)
     project(me_l)
+    term_join(pre_b, rs1, rs1_sem)
     cnt_copies = [
         send(cnt.at[me_s], cnt.at[me_s], cnt_sem, (d,), {"seq": p})
         for d, p in enumerate(seq_peers)
     ]
-    total = pre_b[share(me_l), :].astype(F32)
-    for d in reversed(lab_order):
-        copies[d].wait_recv()
-        total = total + rs1[d - 1].astype(F32)
+    total = term_sum(pre_b[share(me_l), :].astype(F32), rs1, rs1_sem)
     lat[share(me_l), :] = jnp.tanh(total).astype(BF16)
     copies = gather_start(lat, ag1_sem)
     loads[2].wait()
@@ -306,13 +366,13 @@
             sg_s[share(j), at] = sg
             acc[...] += nn(sg, queries[at, :]) + nn(vg, codew[at, :])
 
-    rs2_copies = {}
-    for d in lab_order:
+    for d in reduce_order:
         p = lab_peers[d - 1]
         latent_grad(p)
         lg_b[share(p), :] = acc[...].astype(BF16)
-        rs2_copies[d] = send(lg_b.at[share(p)], rs2.at[d - 1], rs2_sem, (d - 1,), {"lab": p})
+        term_send(lg_b, rs2, rs2_sem, d)
     latent_grad(me_l)
+    term_join(lg_b, rs2, rs2_sem)
     code_part(vg_s, pw)
     w_first = stage1(1, pw, w1)
     code_part(sg_s, pq)
@@ -328,10 +388,7 @@
     loss_out[...] = scalars[1 : 1 + notes, :] * factor
     gb_out[...] = bias_grad * factor
 
-    total = acc[...]
-    for d in reversed(lab_order):
-        rs2_copies[d].wait_recv()
-        total = total + rs2[d - 1].astype(F32)
+    total = term_sum(acc[...], rs2, rs2_sem)
     wide = lat[share(me_l), :].astype(F32)
     pg[share(me_l), :] = (total * factor * (1.0 - wide * wide)).astype(BF16)
     ag2_copies = gather_start(pg, ag2_sem)
@@ -398,7 +455,7 @@
         vmem((C, E), BF16),
         dma((4,)),
         vmem((T, E), BF16),
-        vmem((L - 1, sh, E), BF16),
+        vmem((L, sh, E), BF16),
         vmem((T, E), BF16),
         vmem((E, T), BF16),
         vmem((T, C), F32),
@@ -413,7 +470,7 @@
         vmem((T, C), BF16),
         vmem((sh, E), F32),
         vmem((T, E), BF16),
-        vmem((L - 1, sh, E), BF16),
+        vmem((L, sh, E), BF16),
         vmem((T, E), BF16),
         vmem((E, T), BF16),
         vmem((C, E), BF16),
@@ -431,9 +488,9 @@
         dma((2, S - 1)),
         dma((2, S - 1)),
         dma((2, L - 1)),
-        dma((2, L - 1)),
         dma((2, L)),
-        dma((2, L - 1)),
+        dma((2, L)),
+        dma((2, L)),
         dma((2, L)),
         dma((2, 3, X)),
         dma((2, 3, X - 1)),

time: 62.5 us -> 65.2 us (1.043)
  the two profiles are of different devices: /device:TPU:0 before, /device:TPU:18 now
where the time goes in v4:
time: 65.2 us; the launch traced here: 65 us
  Pallas kernels  64.3 us (99%)
    pallas_call x1, Pallas kernels, per_device(): pl.pallas_call(functools.partial(kernel, S, L, float(C * L)), out_shape=(...  60.7 us
    pallas_call x1, Pallas kernels, per_device(): pl.pallas_call(finish_kernel, out_shape=(jax.ShapeDtypeStruct((notes,), F...  3.66 us

profile of v4, /device:TPU:18, one launch (start us, length us, event | category | flops | bytes accessed | tf_op | source)
XLA Modules:
  0.0 65.0 jit_solution(329624890120074708)
XLA Ops:
  0.6 60.7 %shard_map.118 = (f32[2,128]{1,0:T(2,128)}, bf16[768,256]{1,0:T(8,128)(2,1)}, bf16[256,256]{1,0:T(8,128)(2,1)}, bf16[576,256]{1,0:T(8,128)(2,1)}, bf16[576,256]{1,0:T(8,128)(2,1)}, /*index=5*/f32[1,2304]{1,0:T(1,128)}) custom-call(bf16[768,1024]{1,0:T(8,128)(2,1)} %hidden_h.1, bf16[1024,256]{1,0:T(8,128)(2,1)} %proj.1, bf16[2304,256]{1,0:T(8,128)(2,1)} %queries_h.1, ...), custom_call_target="tpu_custom_call" | custom-call | tf_op jit(solution)/shard_map/pallas_call | solution.py:505
  61.3 3.7 %shard_map.119 = (f32[2]{0:T(128)}, bf16[768,1024]{1,0:T(8,128)(2,1)}, bf16[256,256]{1,0:T(8,128)(2,1)}, bf16[576,256]{1,0:T(8,128)(2,1)}, bf16[576,256]{1,0:T(8,128)(2,1)}, /*index=5*/f32[2304]{0:T(1024)}) custom-call(f32[2,128]{1,0:T(2,128)} %get-tuple-element.12.loss, bf16[768,256]{1,0:T(8,128)(2,1)} %get-tuple-element.13.pg, ...), custom_call_target="tpu_custom_call" | custom-call | tf_op jit(solution)/shard_map/pallas_call | solution.py:520

commit v5 on v3

--- a/solution.py
+++ b/solution.py
@@ -341,15 +341,23 @@
         if d == 2:
             relay(pg, ag2_sem)
     pgT[...] = pg[...].astype(F32).T.astype(BF16)
-    td = tile_of(D, 256)
-
-    @pl.loop(0, D // td)
-    def _(i):
-        at = rows(i * td, td, td)
+    td = D // S if (D // S) % 128 == 0 else D
+
+    def proj_part(start):
+        at = rows(start, td, td)
         pp[at, :] = nn(pgT[...], hidden[:, at]).T.astype(BF16)
 
-    p_first = stage1(2, pp, p1)
-
+    if td == D:
+        proj_part(0)
+        p_first = stage1(2, pp, p1)
+    else:
+        p_first = {}
+        for d in slots:
+            k = xs[d] * 2 + (1 - c)
+            proj_part(k * td)
+            p_first[d] = send(pp.at[chunk(pp, k)], p1.at[d], st1_sem, (2, d), sister)
+        for d in slots:
+            proj_part((xs[d] * 2 + c) * td)
     pg_out[...] = pg[...]
     p_second = stage2(2, pp, p1, ps, p2, p_first)
     finish(pw, w1, w2, w_first, w_second, factor, gw_out)

time: 62.5 us -> 62.5 us (level)
  no operation moved by 1% of the time
where the time goes in v5:
time: 62.5 us; the launch traced here: 62.3 us
  Pallas kernels  61.7 us (99%)
  between operations  0.64 us (1%)
    pallas_call x1, Pallas kernels, per_device(): pl.pallas_call(functools.partial(kernel, S, L, float(C * L)), out_shape=(...  58 us
    pallas_call x1, Pallas kernels, per_device(): pl.pallas_call(finish_kernel, out_shape=(jax.ShapeDtypeStruct((notes,), F...  3.66 us

profile of v5, /device:TPU:0, one launch (start us, length us, event | category | flops | bytes accessed | tf_op | source)
XLA Modules:
  0.0 62.3 jit_solution(9967996481973814712)
XLA Ops:
  0.6 58.0 %shard_map.118 = (f32[2,128]{1,0:T(2,128)}, bf16[768,256]{1,0:T(8,128)(2,1)}, bf16[256,256]{1,0:T(8,128)(2,1)}, bf16[576,256]{1,0:T(8,128)(2,1)}, bf16[576,256]{1,0:T(8,128)(2,1)}, /*index=5*/f32[1,2304]{1,0:T(1,128)}) custom-call(bf16[768,1024]{1,0:T(8,128)(2,1)} %hidden_h.1, bf16[1024,256]{1,0:T(8,128)(2,1)} %proj.1, bf16[2304,256]{1,0:T(8,128)(2,1)} %queries_h.1, ...), custom_call_target="tpu_custom_call" | custom-call | tf_op jit(solution)/shard_map/pallas_call | solution.py:456
  58.6 3.7 %shard_map.119 = (f32[2]{0:T(128)}, bf16[768,1024]{1,0:T(8,128)(2,1)}, bf16[256,256]{1,0:T(8,128)(2,1)}, bf16[576,256]{1,0:T(8,128)(2,1)}, bf16[576,256]{1,0:T(8,128)(2,1)}, /*index=5*/f32[2304]{0:T(1024)}) custom-call(f32[2,128]{1,0:T(2,128)} %get-tuple-element.12.loss, bf16[768,256]{1,0:T(8,128)(2,1)} %get-tuple-element.13.pg, ...), custom_call_target="tpu_custom_call" | custom-call | tf_op jit(solution)/shard_map/pallas_call | solution.py:471
